TPU v7x, 256 devices: a whole 4x4x8 slice. The times are simulated.
256 devices in a mesh: aux: 16 (over x, y), occ: 16 (over z, core).
Axes of the slice: x: 4, y: 4, z: 8, core: 2. Of those that a mesh axis runs over, the one named last changes fastest.
Arguments:
- integrals: bfloat16 [32, 384, 128, 128], P('aux', 'occ'), may hold values from -1.5 to 1.5
- coefficients: bfloat16 [4096, 384], P('occ'), may hold values from -0.21875 to 0.21875
- pair_rows: int32 [16, 384], P('aux', 'occ'), may hold values from 0 to 1
- pair_cols: int32 [16, 384], P('aux', 'occ'), may hold values from 0 to 31
- pair_count: int32 [16, 16], P('aux', 'occ'), may hold values from 1 to 24, as said below
- row_blocks: int32 [32], replicated, may hold values from 0 to 31, each once
Outputs:
- exchange_matrix: float32 [4096, 4096], P('aux', 'occ')
Inputs may be any that keep to these rules, and one draw needn't show every extreme that they name: `pair_count`: at most 24 live slots for each auxiliary block and row owner, and some auxiliary block and owner has exactly 24.
All inputs are finite; a program needn't handle non-finite values.
Results may differ from a plain program's by a relative error of at most 0.0022.
Values may be sent and summed in bfloat16 or wider, within the bound.
A program may use at most 64 MiB of HBM per device.

v0:
```python
import jax
import jax.numpy as jnp
from jax import lax
from jax.sharding import PartitionSpec as P


def contract_rows(first, second):
    return jnp.einsum("pni,pmi->nm", first, second, preferred_element_type=jnp.float32)


def local(integrals, coefficients, pair_rows, pair_cols, pair_count, row_blocks):
    aux_count = integrals.shape[0]
    block_size = integrals.shape[2]
    block_total = row_blocks.shape[0]
    occ_size = lax.axis_size("occ")
    own_blocks = block_total // occ_size
    strip_width = own_blocks * block_size
    full_coeff = lax.all_gather(coefficients, "occ", axis=0, tiled=True)
    orbitals = full_coeff.shape[1]
    coeff_blocks = full_coeff.reshape(block_total, block_size, orbitals)

    def add_pair(slot_index, partial_half):
        row_slot = pair_rows[0, slot_index]
        basis_block = row_blocks[pair_cols[0, slot_index]]
        coeff_piece = lax.dynamic_index_in_dim(coeff_blocks, basis_block, 0, keepdims=False)
        integral_piece = lax.dynamic_index_in_dim(integrals, slot_index, 1, keepdims=False)
        product = jnp.einsum(
            "pmn,ni->pmi", integral_piece, coeff_piece, preferred_element_type=jnp.float32
        )
        current = lax.dynamic_index_in_dim(partial_half, row_slot, 1, keepdims=False)
        return lax.dynamic_update_index_in_dim(partial_half, current + product, row_slot, 1)

    start_half = jnp.zeros((aux_count, own_blocks, block_size, orbitals), jnp.float32)
    summed_half = lax.fori_loop(0, pair_count[0, 0], add_pair, start_half)
    half = summed_half.reshape(aux_count, strip_width, orbitals).astype(jnp.bfloat16)
    strip = contract_rows(lax.all_gather(half, "occ", axis=1, tiled=True), half)
    summed = lax.psum(strip, "aux")
    share_rows = summed.shape[0] // lax.axis_size("aux")
    mine = lax.dynamic_slice_in_dim(summed, lax.axis_index("aux") * share_rows, share_rows, 0)
    return mine


def solution(mesh):
    return jax.shard_map(
        local,
        mesh=mesh,
        in_specs=(
            P("aux", "occ", None, None),
            P("occ", None),
            P("aux", "occ"),
            P("aux", "occ"),
            P("aux", "occ"),
            P(),
        ),
        out_specs=P("aux", "occ"),
        check_vma=False,
    )
```

profile of v0, /device:TPU:1, one launch (start us, length us, event | category | flops | bytes accessed | tf_op | source)
XLA Modules:
  0.0 470.6 jit_solution(8826988646007465637)
XLA Ops:
  7.3 47.1 %all-gather.3.cloned.1.call-done = bf16[4096,384]{1,0:T(8,128)(2,1)} async-done(((bf16[256,384]{1,0:T(8,128)(2,1)}), bf16[4096,384]{1,0:T(8,128)(2,1)}) %all-gather.3.cloned.1.call-update) | async-done | bytes 3145744 | tf_op jit(solution)/shard_map/all_gather | solution.py:18
  54.5 142.6 %while.10 = (s32[]{:T(128)}, f32[2,2,128,384]{3,2,0,1:T(8,128)S(1)}, s32[]{:T(128)}, s32[1,24]{1,0:T(1,128)}, bf16[2,24,128,128]{3,2,1,0:T(8,128)(2,1)}, /*index...) while((s32[]{:T(128)}, ...), condition=%wide.region_1.2_spmd, body=%wide.region_0.1_spmd.sunk | while | flops 25264140 | bytes 1737021 | solution.py:34
  55.1 1.3 constant_dynamic-slice_fusion.6
  60.3 1.3 dynamic_slice.46
  65.3 1.3 constant_dynamic-slice_fusion.6
  70.4 1.3 dynamic_slice.46
  75.4 1.3 constant_dynamic-slice_fusion.6
  80.6 1.3 dynamic_slice.46
  85.6 1.3 constant_dynamic-slice_fusion.6
  90.7 1.3 dynamic_slice.46
  95.7 1.3 constant_dynamic-slice_fusion.6
  100.8 1.3 dynamic_slice.46
  105.8 1.3 constant_dynamic-slice_fusion.6
  111.0 1.3 dynamic_slice.46
  116.0 1.3 constant_dynamic-slice_fusion.6
  121.1 1.3 dynamic_slice.46
  126.1 1.3 constant_dynamic-slice_fusion.6
  131.3 1.3 dynamic_slice.46
  136.3 1.3 constant_dynamic-slice_fusion.6
  141.4 1.3 dynamic_slice.46
  146.4 1.3 constant_dynamic-slice_fusion.6
  151.6 1.3 dynamic_slice.46
  156.5 1.3 constant_dynamic-slice_fusion.6
  161.7 1.3 dynamic_slice.46
  166.7 1.3 constant_dynamic-slice_fusion.6
  176.8 1.3 constant_dynamic-slice_fusion.6
  182.0 1.3 dynamic_slice.46
  187.0 1.3 constant_dynamic-slice_fusion.6
  198.0 145.8 %all-gather.5.cloned.1.call-done = bf16[2,4096,384]{2,1,0:T(8,128)(2,1)} async-done(((bf16[2,256,384]{2,1,0:T(8,128)(2,1)}), bf16[2,4096,384]{2,1,0:T(8,128)(2,1)}) %all-gather.5.cloned.1.call-update) | async-done | bytes 6291472 | tf_op jit(solution)/shard_map/all_gather | solution.py:36
  343.8 6.7 %convolution_bitcast_fusion = f32[4096,256]{1,0:T(8,128)} fusion(bf16[2,4096,384]{2,1,0:T(8,128)(2,1)} %all-gather.5.cloned.1.call-done, bf16[2,256,384]{2,1,0:T(8,128)(2,1)} %bitcast.40), kind=kOutput, calls=%fused_computation.11 | convolution fusion | flops 1610612736 | bytes 10878976 | tf_op jit(solution)/shard_map/pni,pmi->nm/dot_general | solution.py:8
  350.5 111.8 %all-reduce.2.cloned.1.call-done = f32[4096,256]{1,0:T(8,128)} async-done(((f32[4096,256]{1,0:T(8,128)}), f32[4096,256]{1,0:T(8,128)}) %all-reduce.2.cloned.1.call-update) | async-done | bytes 4194320 | tf_op jit(solution)/shard_map/psum | solution.py:37
  462.4 1.7 constant_dynamic-slice_fusion.3
  (39 shorter events, 20.6 us)
Async XLA Ops:
  6.5 47.9 %all-gather.3.cloned.1.call-start = ((), (), s32[]{:S(2)}) async-start(), calls=%async_computation | async-start | bytes 3342336 | tf_op jit(solution)/shard_map/all_gather | solution.py:18
  7.3 336.6 %all-gather.5.cloned.1.call-start = ((), (), s32[]{:S(2)}) async-start(), calls=%async_computation.1 | async-start | bytes 6684672 | tf_op jit(solution)/shard_map/all_gather | solution.py:36
  198.0 264.4 %all-reduce.2.cloned.1.call-start = ((), (), s32[]{:S(2)}) async-start(), calls=%async_computation.2 | async-start | bytes 8388608 | tf_op jit(solution)/shard_map/psum | solution.py:37
Sparse Core Ops, SparseCore 0:
  9.2 45.1 all-gather.2
  198.1 145.6 all-gather.4
  350.6 111.6 all-reduce.1
where the time goes:
time: 474 us; the launch traced here: 471 us
  waiting for transfers between devices  305 us (64%)
  loops' own time  90.1 us (19%)
  local copies, waits for them, and re-layouts  39.1 us (8%)
  matrix products  22.6 us (5%)
  between operations  13.1 us (3%)
    all_gather x1, waiting for transfers between devices, local(): strip = contract_rows(lax.all_gather(half, 'occ', axis=1, tiled=True), half)  146 us
    psum x1, waiting for transfers between devices, local(): summed = lax.psum(strip, 'aux')  112 us
    another operation x1, loops' own time, local(): summed_half = lax.fori_loop(0, pair_count[0, 0], add_pair, start_half)  90.1 us
    all_gather x1, waiting for transfers between devices, local(): full_coeff = lax.all_gather(coefficients, 'occ', axis=0, tiled=True)  47.1 us
    dynamic_slice x28, local copies, waits for them, and re-layouts, add_pair(): basis_block = row_blocks[pair_cols[0, slot_index]]  36.1 us
    dot_general x14, matrix products, add_pair(): jnp.einsum('pmn,ni->pmi', integral_piece, coeff_piece, preferred_element_...  15.9 us
  transfers between devices with their start and end apart: 3, of which 3 were waited for; matrix products, arithmetic and copies ran while one was open for 0% of the time, Pallas kernels for 0%

commit v1 on v0

--- a/solution.py
+++ b/solution.py
@@ -2,6 +2,27 @@
 import jax.numpy as jnp
 from jax import lax
 from jax.sharding import PartitionSpec as P
+
+
+def gather_around(shard, axis, dim):
+    peers, mine, extent = (lax.axis_size(axis), lax.axis_index(axis), shard.shape[dim])
+    upward = [(i, (i + 1) % peers) for i in range(peers)]
+    left = [(i, (i - 1) % peers) for i in range(peers)]
+    filled = jnp.zeros((*shard.shape[:dim], peers * extent, *shard.shape[dim + 1 :]), shard.dtype)
+    filled = lax.dynamic_update_slice_in_dim(filled, shard, mine * extent, axis=dim)
+    from_left = from_right = shard
+    half = peers // 2
+    for step in range(1, half + 1):
+        from_left = lax.ppermute(from_left, axis, upward)
+        filled = lax.dynamic_update_slice_in_dim(
+            filled, from_left, (mine - step) % peers * extent, axis=dim
+        )
+        if step < peers - half:
+            from_right = lax.ppermute(from_right, axis, left)
+            filled = lax.dynamic_update_slice_in_dim(
+                filled, from_right, (mine + step) % peers * extent, axis=dim
+            )
+    return filled
 
 
 def contract_rows(first, second):
@@ -33,7 +54,7 @@
     start_half = jnp.zeros((aux_count, own_blocks, block_size, orbitals), jnp.float32)
     summed_half = lax.fori_loop(0, pair_count[0, 0], add_pair, start_half)
     half = summed_half.reshape(aux_count, strip_width, orbitals).astype(jnp.bfloat16)
-    strip = contract_rows(lax.all_gather(half, "occ", axis=1, tiled=True), half)
+    strip = contract_rows(gather_around(half, "occ", 1), half)
     summed = lax.psum(strip, "aux")
     share_rows = summed.shape[0] // lax.axis_size("aux")
     mine = lax.dynamic_slice_in_dim(summed, lax.axis_index("aux") * share_rows, share_rows, 0)

time: 474 us -> 480 us (1.013)
  starting transfers between devices: 0.08 us -> 107 us
  waiting for transfers between devices: 305 us -> 210 us
    all_gather x1 -> x0, waiting for transfers between devices: 146 us -> none  [local(): strip = contract_rows(lax.all_gather(half, 'occ', axis=1, tiled=True), half)]
    ppermute x0 -> x15, starting transfers between devices: none -> 107 us  [the longest x8 62.5 us: gather_around(): from_left = lax.ppermute(from_left, axis, upward)]
    psum x1, waiting for transfers between devices: 112 us -> 143 us  [local(): summed = lax.psum(strip, 'aux')]
    ppermute x0 -> x15, waiting for transfers between devices: none -> 19.1 us  [the longest x8 16.1 us: gather_around(): from_left = lax.ppermute(from_left, axis, upward)]
  transfers between devices with their start and end apart: 3 -> 17, of which waited for: 3 -> 15; matrix products, arithmetic and copies ran while one was open for 0% -> 0% of each run, Pallas kernels for 0% -> 0%
where the time goes in v1:
time: 480 us; the launch traced here: 476 us
  waiting for transfers between devices  210 us (44%)
  starting transfers between devices  107 us (22%)
  loops' own time  86.2 us (18%)
  local copies, waits for them, and re-layouts  39.6 us (8%)
  matrix products  19.8 us (4%)
  between operations  13.5 us (3%)
    psum x1, waiting for transfers between devices, local(): summed = lax.psum(strip, 'aux')  143 us
    another operation x1, loops' own time, local(): summed_half = lax.fori_loop(0, pair_count[0, 0], add_pair, start_half)  86.2 us
    ppermute x8, starting transfers between devices, gather_around(): from_left = lax.ppermute(from_left, axis, upward)  62.5 us
    all_gather x1, waiting for transfers between devices, local(): full_coeff = lax.all_gather(coefficients, 'occ', axis=0, tiled=True)  47.1 us
    ppermute x7, starting transfers between devices, gather_around(): from_right = lax.ppermute(from_right, axis, left)  44.2 us
    dynamic_slice x28, local copies, waits for them, and re-layouts, add_pair(): basis_block = row_blocks[pair_cols[0, slot_index]]  35.5 us
    ppermute x8, waiting for transfers between devices, gather_around(): from_left = lax.ppermute(from_left, axis, upward)  16.1 us
    dot_general x14, matrix products, add_pair(): jnp.einsum('pmn,ni->pmi', integral_piece, coeff_piece, preferred_element_...  15.9 us
  transfers between devices with their start and end apart: 17, of which 15 were waited for; matrix products, arithmetic and copies ran while one was open for 0% of the time, Pallas kernels for 0%

profile of v1, /device:TPU:1, one launch (start us, length us, event | category | flops | bytes accessed | tf_op | source)
XLA Modules:
  0.0 476.2 jit_solution(13779007367232960431)
XLA Ops:
  7.3 47.1 %all-gather.2.cloned.1.call-done = bf16[4096,384]{1,0:T(8,128)(2,1)} async-done(((bf16[256,384]{1,0:T(8,128)(2,1)}), bf16[4096,384]{1,0:T(8,128)(2,1)}) %all-gather.2.cloned.1.call-update) | async-done | bytes 3145744 | tf_op jit(solution)/shard_map/all_gather | solution.py:39
  54.5 138.1 %while.10 = (s32[]{:T(128)}, f32[2,2,128,384]{3,2,1,0:T(8,128)S(1)}, s32[]{:T(128)}, s32[1,24]{1,0:T(1,128)}, bf16[2,24,128,128]{3,2,1,0:T(8,128)(2,1)}, /*index...) while((s32[]{:T(128)}, ...), condition=%wide.region_1.2_spmd, body=%wide.region_0.1_spmd.sunk | while | flops 25264140 | bytes 1737013 | solution.py:55
  55.1 1.3 constant_dynamic-slice_fusion.6
  60.0 1.3 dynamic_slice.46
  65.0 1.3 constant_dynamic-slice_fusion.6
  69.8 1.3 dynamic_slice.46
  74.8 1.3 constant_dynamic-slice_fusion.6
  84.6 1.3 constant_dynamic-slice_fusion.6
  94.4 1.3 constant_dynamic-slice_fusion.6
  104.2 1.3 constant_dynamic-slice_fusion.6
  109.1 1.3 dynamic_slice.46
  114.1 1.3 constant_dynamic-slice_fusion.6
  123.9 1.3 constant_dynamic-slice_fusion.6
  133.7 1.3 constant_dynamic-slice_fusion.6
  143.5 1.3 constant_dynamic-slice_fusion.6
  153.3 1.3 constant_dynamic-slice_fusion.6
  163.1 1.3 constant_dynamic-slice_fusion.6
  173.0 1.3 constant_dynamic-slice_fusion.6
  182.8 1.3 constant_dynamic-slice_fusion.6
  192.6 60.0 %collective-permute-start = (bf16[2,256,384]{2,1,0:T(8,128)(2,1)S(1)}, bf16[2,256,384]{2,1,0:T(8,128)(2,1)S(1)}, u32[]{:S(2)}, u32[]{:S(2)}) collective-permute-start(bf16[2,256,384]{2,1,0:T(8,128)(2,1)S(1)} %bitcast.43), channel_id=1, source_target_pairs={{0,1},{1,2},{2,3},{3,4},{4,5},{5,6},{6,7},{7,8},{8,9},{9,10},{10,1... | collective-permute-start | bytes 1179656 | tf_op jit(solution)/shard_map/ppermute | solution.py:16
  252.7 4.7 collective-permute-done
  257.4 2.5 collective-permute-start.2
  259.9 8.9 %collective-permute-start.3 = (bf16[2,256,384]{2,1,0:T(8,128)(2,1)S(1)}, bf16[2,256,384]{2,1,0:T(8,128)(2,1)S(1)}, u32[]{:S(2)}, u32[]{:S(2)}) collective-permute-start(bf16[2,256,384]{2,1,0:T(8,128)(2,1)S(1)} %collective-permute-done.1), channel_id=1, source_target_pairs={{0,15},{1,0},{2,1},{3,2},{4,3},{5,4},{6,5},{7,6},{8,7},{9,8},{10,9... | collective-permute-start | bytes 1179656 | tf_op jit(solution)/shard_map/ppermute | solution.py:21
  270.2 7.0 %collective-permute-start.5 = (bf16[2,256,384]{2,1,0:T(8,128)(2,1)S(1)}, bf16[2,256,384]{2,1,0:T(8,128)(2,1)S(1)}, u32[]{:S(2)}, u32[]{:S(2)}) collective-permute-start(bf16[2,256,384]{2,1,0:T(8,128)(2,1)S(1)} %collective-permute-done.3), channel_id=1, source_target_pairs={{0,15},{1,0},{2,1},{3,2},{4,3},{5,4},{6,5},{7,6},{8,7},{9,8},{10,9... | collective-permute-start | bytes 1179656 | tf_op jit(solution)/shard_map/ppermute | solution.py:21
  278.6 7.1 %collective-permute-start.7 = (bf16[2,256,384]{2,1,0:T(8,128)(2,1)S(1)}, bf16[2,256,384]{2,1,0:T(8,128)(2,1)S(1)}, u32[]{:S(2)}, u32[]{:S(2)}) collective-permute-start(bf16[2,256,384]{2,1,0:T(8,128)(2,1)S(1)} %collective-permute-done.5), channel_id=1, source_target_pairs={{0,15},{1,0},{2,1},{3,2},{4,3},{5,4},{6,5},{7,6},{8,7},{9,8},{10,9... | collective-permute-start | bytes 1179656 | tf_op jit(solution)/shard_map/ppermute | solution.py:21
  287.9 7.2 %collective-permute-start.9 = (bf16[2,256,384]{2,1,0:T(8,128)(2,1)S(1)}, bf16[2,256,384]{2,1,0:T(8,128)(2,1)S(1)}, u32[]{:S(2)}, u32[]{:S(2)}) collective-permute-start(bf16[2,256,384]{2,1,0:T(8,128)(2,1)S(1)} %collective-permute-done.7), channel_id=1, source_target_pairs={{0,15},{1,0},{2,1},{3,2},{4,3},{5,4},{6,5},{7,6},{8,7},{9,8},{10,9... | collective-permute-start | bytes 1179656 | tf_op jit(solution)/shard_map/ppermute | solution.py:21
  296.5 6.9 %collective-permute-start.11 = (bf16[2,256,384]{2,1,0:T(8,128)(2,1)S(1)}, bf16[2,256,384]{2,1,0:T(8,128)(2,1)S(1)}, u32[]{:S(2)}, u32[]{:S(2)}) collective-permute-start(bf16[2,256,384]{2,1,0:T(8,128)(2,1)S(1)} %collective-permute-done.9), channel_id=1, source_target_pairs={{0,15},{1,0},{2,1},{3,2},{4,3},{5,4},{6,5},{7,6},{8,7},{9,8},{10,9... | collective-permute-start | bytes 1179656 | tf_op jit(solution)/shard_map/ppermute | solution.py:21
  304.7 7.1 %collective-permute-start.13 = (bf16[2,256,384]{2,1,0:T(8,128)(2,1)S(1)}, bf16[2,256,384]{2,1,0:T(8,128)(2,1)S(1)}, u32[]{:S(2)}, u32[]{:S(2)}) collective-permute-start(bf16[2,256,384]{2,1,0:T(8,128)(2,1)S(1)} %collective-permute-done.11), channel_id=1, source_target_pairs={{0,15},{1,0},{2,1},{3,2},{4,3},{5,4},{6,5},{7,6},{8,7},{9,8},{10,9... | collective-permute-start | bytes 1179656 | tf_op jit(solution)/shard_map/ppermute | solution.py:21
  313.2 7.3 %collective-permute-done.14 = bf16[2,256,384]{2,1,0:T(8,128)(2,1)S(1)} collective-permute-done((bf16[2,256,384]{2,1,0:T(8,128)(2,1)S(1)}, bf16[2,256,384]{2,1,0:T(8,128)(2,1)S(1)}, u32[]{:S(2)}, u32[]{:S(2)}) %collective-permute-start.14) | collective-permute-done | bytes 393248 | tf_op jit(solution)/shard_map/ppermute | solution.py:16
  320.6 3.9 convolution_bitcast_fusion
  324.5 143.3 %all-reduce.2.cloned.1.call-done = f32[4096,256]{1,0:T(8,128)} async-done(((f32[4096,256]{1,0:T(8,128)}), f32[4096,256]{1,0:T(8,128)}) %all-reduce.2.cloned.1.call-update) | async-done | bytes 4194320 | tf_op jit(solution)/shard_map/psum | solution.py:58
  467.7 1.7 constant_dynamic-slice_fusion.3
  (86 shorter events, 40.2 us)
Async XLA Ops:
  6.5 47.9 %all-gather.2.cloned.1.call-start = ((), (), s32[]{:S(2)}) async-start(), calls=%async_computation | async-start | bytes 3342336 | tf_op jit(solution)/shard_map/all_gather | solution.py:39
  7.3 460.5 %all-reduce.2.cloned.1.call-start = ((), (), s32[]{:S(2)}) async-start(), calls=%async_computation.1 | async-start | bytes 8388608 | tf_op jit(solution)/shard_map/psum | solution.py:58
  192.6 64.8 %collective-permute-start = (bf16[2,256,384]{2,1,0:T(8,128)(2,1)S(1)}, bf16[2,256,384]{2,1,0:T(8,128)(2,1)S(1)}, u32[]{:S(2)}, u32[]{:S(2)}) collective-permute-start(bf16[2,256,384]{2,1,0:T(8,128)(2,1)S(1)} %bitcast.43), channel_id=1, source_target_pairs={{0,1},{1,2},{2,3},{3,4},{4,5},{5,6},{6,7},{7,8},{8,9},{9,10},{10,1... | collective-permute-start | bytes 1179656 | tf_op jit(solution)/shard_map/ppermute | solution.py:16
  252.7 7.2 %collective-permute-start.1 = (bf16[2,256,384]{2,1,0:T(8,128)(2,1)S(1)}, bf16[2,256,384]{2,1,0:T(8,128)(2,1)S(1)}, u32[]{:S(2)}, u32[]{:S(2)}) collective-permute-start(bf16[2,256,384]{2,1,0:T(8,128)(2,1)S(1)} %bitcast.44), channel_id=1, source_target_pairs={{0,15},{1,0},{2,1},{3,2},{4,3},{5,4},{6,5},{7,6},{8,7},{9,8},{10,9... | collective-permute-start | bytes 1179656 | tf_op jit(solution)/shard_map/ppermute | solution.py:21
  257.4 19.8 %copy-start = (bf16[2,256,384]{2,1,0:T(8,128)(2,1)}, bf16[2,256,384]{2,1,0:T(8,128)(2,1)S(1)}, u32[]{:S(2)}) copy-start(bf16[2,256,384]{2,1,0:T(8,128)(2,1)S(1)} %collective-permute-done) | copy-start | bytes 1179652
  257.4 12.6 %collective-permute-start.2 = (bf16[2,256,384]{2,1,0:T(8,128)(2,1)S(1)}, bf16[2,256,384]{2,1,0:T(8,128)(2,1)S(1)}, u32[]{:S(2)}, u32[]{:S(2)}) collective-permute-start(bf16[2,256,384]{2,1,0:T(8,128)(2,1)S(1)} %collective-permute-done), channel_id=1, source_target_pairs={{0,1},{1,2},{2,3},{3,4},{4,5},{5,6},{6,7},{7,8},{8,9},{9,10},{10,1... | collective-permute-start | bytes 1179656 | tf_op jit(solution)/shard_map/ppermute | solution.py:16
  259.9 10.3 %collective-permute-start.3 = (bf16[2,256,384]{2,1,0:T(8,128)(2,1)S(1)}, bf16[2,256,384]{2,1,0:T(8,128)(2,1)S(1)}, u32[]{:S(2)}, u32[]{:S(2)}) collective-permute-start(bf16[2,256,384]{2,1,0:T(8,128)(2,1)S(1)} %collective-permute-done.1), channel_id=1, source_target_pairs={{0,15},{1,0},{2,1},{3,2},{4,3},{5,4},{6,5},{7,6},{8,7},{9,8},{10,9... | collective-permute-start | bytes 1179656 | tf_op jit(solution)/shard_map/ppermute | solution.py:21
  270.0 8.4 %collective-permute-start.4 = (bf16[2,256,384]{2,1,0:T(8,128)(2,1)S(1)}, bf16[2,256,384]{2,1,0:T(8,128)(2,1)S(1)}, u32[]{:S(2)}, u32[]{:S(2)}) collective-permute-start(bf16[2,256,384]{2,1,0:T(8,128)(2,1)S(1)} %collective-permute-done.2), channel_id=1, source_target_pairs={{0,1},{1,2},{2,3},{3,4},{4,5},{5,6},{6,7},{7,8},{8,9},{9,10},{10,1... | collective-permute-start | bytes 1179656 | tf_op jit(solution)/shard_map/ppermute | solution.py:16
  270.2 8.4 %collective-permute-start.5 = (bf16[2,256,384]{2,1,0:T(8,128)(2,1)S(1)}, bf16[2,256,384]{2,1,0:T(8,128)(2,1)S(1)}, u32[]{:S(2)}, u32[]{:S(2)}) collective-permute-start(bf16[2,256,384]{2,1,0:T(8,128)(2,1)S(1)} %collective-permute-done.3), channel_id=1, source_target_pairs={{0,15},{1,0},{2,1},{3,2},{4,3},{5,4},{6,5},{7,6},{8,7},{9,8},{10,9... | collective-permute-start | bytes 1179656 | tf_op jit(solution)/shard_map/ppermute | solution.py:21
  278.4 8.4 %collective-permute-start.6 = (bf16[2,256,384]{2,1,0:T(8,128)(2,1)S(1)}, bf16[2,256,384]{2,1,0:T(8,128)(2,1)S(1)}, u32[]{:S(2)}, u32[]{:S(2)}) collective-permute-start(bf16[2,256,384]{2,1,0:T(8,128)(2,1)S(1)} %collective-permute-done.4), channel_id=1, source_target_pairs={{0,1},{1,2},{2,3},{3,4},{4,5},{5,6},{6,7},{7,8},{8,9},{9,10},{10,1... | collective-permute-start | bytes 1179656 | tf_op jit(solution)/shard_map/ppermute | solution.py:16
  278.6 9.3 %collective-permute-start.7 = (bf16[2,256,384]{2,1,0:T(8,128)(2,1)S(1)}, bf16[2,256,384]{2,1,0:T(8,128)(2,1)S(1)}, u32[]{:S(2)}, u32[]{:S(2)}) collective-permute-start(bf16[2,256,384]{2,1,0:T(8,128)(2,1)S(1)} %collective-permute-done.5), channel_id=1, source_target_pairs={{0,15},{1,0},{2,1},{3,2},{4,3},{5,4},{6,5},{7,6},{8,7},{9,8},{10,9... | collective-permute-start | bytes 1179656 | tf_op jit(solution)/shard_map/ppermute | solution.py:21
  286.9 8.4 %collective-permute-start.8 = (bf16[2,256,384]{2,1,0:T(8,128)(2,1)S(1)}, bf16[2,256,384]{2,1,0:T(8,128)(2,1)S(1)}, u32[]{:S(2)}, u32[]{:S(2)}) collective-permute-start(bf16[2,256,384]{2,1,0:T(8,128)(2,1)S(1)} %collective-permute-done.6), channel_id=1, source_target_pairs={{0,1},{1,2},{2,3},{3,4},{4,5},{5,6},{6,7},{7,8},{8,9},{9,10},{10,1... | collective-permute-start | bytes 1179656 | tf_op jit(solution)/shard_map/ppermute | solution.py:16
  286.9 1.0 copy-start.1
  287.9 8.6 %collective-permute-start.9 = (bf16[2,256,384]{2,1,0:T(8,128)(2,1)S(1)}, bf16[2,256,384]{2,1,0:T(8,128)(2,1)S(1)}, u32[]{:S(2)}, u32[]{:S(2)}) collective-permute-start(bf16[2,256,384]{2,1,0:T(8,128)(2,1)S(1)} %collective-permute-done.7), channel_id=1, source_target_pairs={{0,15},{1,0},{2,1},{3,2},{4,3},{5,4},{6,5},{7,6},{8,7},{9,8},{10,9... | collective-permute-start | bytes 1179656 | tf_op jit(solution)/shard_map/ppermute | solution.py:21
  295.3 8.4 %collective-permute-start.10 = (bf16[2,256,384]{2,1,0:T(8,128)(2,1)S(1)}, bf16[2,256,384]{2,1,0:T(8,128)(2,1)S(1)}, u32[]{:S(2)}, u32[]{:S(2)}) collective-permute-start(bf16[2,256,384]{2,1,0:T(8,128)(2,1)S(1)} %collective-permute-done.8), channel_id=1, source_target_pairs={{0,1},{1,2},{2,3},{3,4},{4,5},{5,6},{6,7},{7,8},{8,9},{9,10},{10,1... | collective-permute-start | bytes 1179656 | tf_op jit(solution)/shard_map/ppermute | solution.py:16
  296.5 8.2 %collective-permute-start.11 = (bf16[2,256,384]{2,1,0:T(8,128)(2,1)S(1)}, bf16[2,256,384]{2,1,0:T(8,128)(2,1)S(1)}, u32[]{:S(2)}, u32[]{:S(2)}) collective-permute-start(bf16[2,256,384]{2,1,0:T(8,128)(2,1)S(1)} %collective-permute-done.9), channel_id=1, source_target_pairs={{0,15},{1,0},{2,1},{3,2},{4,3},{5,4},{6,5},{7,6},{8,7},{9,8},{10,9... | collective-permute-start | bytes 1179656 | tf_op jit(solution)/shard_map/ppermute | solution.py:21
  303.7 8.4 %collective-permute-start.12 = (bf16[2,256,384]{2,1,0:T(8,128)(2,1)S(1)}, bf16[2,256,384]{2,1,0:T(8,128)(2,1)S(1)}, u32[]{:S(2)}, u32[]{:S(2)}) collective-permute-start(bf16[2,256,384]{2,1,0:T(8,128)(2,1)S(1)} %collective-permute-done.10), channel_id=1, source_target_pairs={{0,1},{1,2},{2,3},{3,4},{4,5},{5,6},{6,7},{7,8},{8,9},{9,10},{10,1... | collective-permute-start | bytes 1179656 | tf_op jit(solution)/shard_map/ppermute | solution.py:16
  304.7 8.4 %collective-permute-start.13 = (bf16[2,256,384]{2,1,0:T(8,128)(2,1)S(1)}, bf16[2,256,384]{2,1,0:T(8,128)(2,1)S(1)}, u32[]{:S(2)}, u32[]{:S(2)}) collective-permute-start(bf16[2,256,384]{2,1,0:T(8,128)(2,1)S(1)} %collective-permute-done.11), channel_id=1, source_target_pairs={{0,15},{1,0},{2,1},{3,2},{4,3},{5,4},{6,5},{7,6},{8,7},{9,8},{10,9... | collective-permute-start | bytes 1179656 | tf_op jit(solution)/shard_map/ppermute | solution.py:21
  312.1 8.4 %collective-permute-start.14 = (bf16[2,256,384]{2,1,0:T(8,128)(2,1)S(1)}, bf16[2,256,384]{2,1,0:T(8,128)(2,1)S(1)}, u32[]{:S(2)}, u32[]{:S(2)}) collective-permute-start(bf16[2,256,384]{2,1,0:T(8,128)(2,1)S(1)} %collective-permute-done.12), channel_id=1, source_target_pairs={{0,1},{1,2},{2,3},{3,4},{4,5},{5,6},{6,7},{7,8},{8,9},{9,10},{10,1... | collective-permute-start | bytes 1179656 | tf_op jit(solution)/shard_map/ppermute | solution.py:16
Sparse Core Ops, SparseCore 0:
  9.2 45.1 all-gather.1
  324.6 143.0 all-reduce.1
